TPU v7x, 32 devices: a whole 2x2x4 slice. The times are simulated.
32 devices in a mesh: dp: 4 (over x, core), ctx: 4 (over z), tensor: 2 (over y).
Axes of the slice: x: 2, y: 2, z: 4, core: 2. Of those that a mesh axis runs over, the one named last changes fastest.
Arguments:
- block_input: bfloat16 [12288, 2048], P(('dp', 'ctx'), 'tensor'), may hold values from -6 to 6
- cotangent: bfloat16 [12288, 2048], P(('dp', 'ctx'), 'tensor'), may hold values from -6 to 6
- deal_order: int32 [4, 4], P('dp'), may hold values from 0 to 3, as said below
- seq_lengths: int32 [12], P('dp'), may hold values from 96 to 2880, as said below
- seq_adapter: int32 [12], P('dp'), may hold values from 0 to 7
- mixer_gain: bfloat16 [2048], replicated, may hold values from 0.099609375 to 1.8984375
- ffn_gain: bfloat16 [2048], replicated, may hold values from 0.099609375 to 1.8984375
- conv_taps: bfloat16 [3, 2048], P(None, 'tensor'), may hold values from -3.5 to 3.5
- in_weight: bfloat16 [3, 2048, 2048], P(None, 'dp', 'tensor'), may hold values from -0.125 to 0.125
- out_weight: bfloat16 [2048, 2048], P('tensor', 'dp'), may hold values from -0.125 to 0.125
- gateup_weight: bfloat16 [2, 2048, 5632], P(None, 'dp', 'tensor'), may hold values from -0.125 to 0.125
- down_weight: bfloat16 [5632, 2048], P('tensor', 'dp'), may hold values from -0.078125 to 0.078125
- input_adapter_shrink: bfloat16 [2048, 128], replicated, may hold values from -0.125 to 0.125
- in_expand: bfloat16 [3, 128, 2048], P(None, None, 'tensor'), may hold values from -1.5 to 1.5
- out_shrink: bfloat16 [2048, 128], P('tensor'), may hold values from -0.125 to 0.125
- output_adapter_expand: bfloat16 [128, 2048], replicated, may hold values from -1.5 to 1.5
- ffn_shrink: bfloat16 [2048, 256], replicated, may hold values from -0.125 to 0.125
- ffn_expand: bfloat16 [2, 128, 5632], P(None, None, 'tensor'), may hold values from -1.5 to 1.5
- down_shrink: bfloat16 [5632, 128], P('tensor'), may hold values from -0.078125 to 0.078125
- down_adapter_expand: bfloat16 [128, 2048], replicated, may hold values from -1.5 to 1.5
Outputs:
- block_output: bfloat16 [12288, 2048], P(('dp', 'ctx'), 'tensor')
- input_grad: float32 [12288, 2048], P(('dp', 'ctx'), 'tensor')
- in_shrink_grad: float32 [2048, 128], replicated
- input_expand_gradient: float32 [3, 128, 2048], P(None, None, 'tensor')
- out_shrink_grad: float32 [2048, 128], P('tensor')
- output_expand_gradient: float32 [128, 2048], replicated
- ffn_shrink_grad: float32 [2048, 256], replicated
- feedforward_expand_gradient: float32 [2, 128, 5632], P(None, None, 'tensor')
- down_shrink_grad: float32 [5632, 128], P('tensor')
- down_adapter_expand_gradient: float32 [128, 2048], replicated
Inputs may be any that keep to these rules, and one draw needn't show every extreme that they name: `deal_order`: each row is a permutation of the 4 shard numbers. `seq_lengths`: each data group's 3 entries sum to 3072; all but one of them lie between 96 and 192.
All inputs are finite; a program needn't handle non-finite values.
Results may differ from a plain program's by a relative error of at most 0.013.
Values may be sent and summed in bfloat16 or wider, within the bound.
No kernel may reach another device: no remote copies, remote signals or barrier semaphores. Data moves between devices by JAX's collectives and lax.ppermute only.
A program may use at most 256 MiB of HBM per device.

v0:
```python
import jax
import jax.numpy as jnp
from jax import lax
from jax.sharding import PartitionSpec as P

RANK = 16
norm_eps = 1e-05
adapter_scale = 0.5


def shifted(block, axis, distance):
    devices = range(lax.axis_size(axis))
    route = [(i - distance, i) for i in devices if i - distance in devices]
    return lax.ppermute(block, axis, route)


def rms_scale(values):
    return lax.rsqrt(jnp.mean(values * values, axis=-1, keepdims=True) + norm_eps)


def norm_back(values, scale, gain, grad_out):
    unit = values * scale
    grad_unit = grad_out * gain
    return scale * (grad_unit - unit * jnp.mean(grad_unit * unit, axis=-1, keepdims=True))


def product_simple(left, right):
    return jnp.dot(left, right, preferred_element_type=jnp.float32)


def product_backward(left, right):
    return lax.dot_general(
        left, right, (((1,), (1,)), ((), ())), preferred_element_type=jnp.float32
    )


def product_leading(left, right):
    return lax.dot_general(
        left, right, (((0,), (0,)), ((), ())), preferred_element_type=jnp.float32
    )


def segment_of(positions, seq_ends):
    return jnp.sum((positions[:, None] >= seq_ends[None, :]).astype(jnp.int32), axis=1)


def fetch_mixer(in_weight, out_weight):
    return (
        lax.all_gather(in_weight, "dp", axis=1, tiled=True),
        lax.all_gather(out_weight, "dp", axis=1, tiled=True),
    )


def fetch_ffn(gateup_weight, down_weight):
    return (
        lax.all_gather(gateup_weight, "dp", axis=1, tiled=True),
        lax.all_gather(down_weight, "dp", axis=1, tiled=True),
    )


def body(
    block_input,
    cotangent,
    deal_order,
    seq_lengths,
    seq_adapter,
    mixer_gain,
    ffn_gain,
    conv_taps,
    in_weight,
    out_weight,
    gateup_weight,
    down_weight,
    input_adapter_shrink,
    in_expand,
    out_shrink,
    output_adapter_expand,
    ffn_shrink,
    ffn_expand,
    down_shrink,
    down_adapter_expand,
):
    tok_count = block_input.shape[0]
    half_width = block_input.shape[1]
    rank_cols = input_adapter_shrink.shape[1]
    part_index = lax.axis_index("tensor")
    group_total = lax.axis_size("dp")
    block_rows = tok_count // group_total
    deal_row = deal_order[0]
    slot_all = jnp.arange(group_total, dtype=jnp.int32)
    inverse_row = jnp.sum(
        jnp.where(deal_row[:, None] == slot_all[None, :], slot_all[:, None], 0), axis=0
    )
    dealt_in, dealt_cot = (
        lax.all_to_all(
            block_input.reshape(group_total, block_rows, half_width),
            "dp",
            split_axis=0,
            concat_axis=0,
            tiled=True,
        ),
        lax.all_to_all(
            cotangent.reshape(group_total, block_rows, half_width),
            "dp",
            split_axis=0,
            concat_axis=0,
            tiled=True,
        ),
    )
    packed_in = jnp.take(dealt_in, deal_row, axis=0).reshape(tok_count, half_width)
    packed_cot = jnp.take(dealt_cot, deal_row, axis=0).reshape(tok_count, half_width)
    seq_ends = jnp.cumsum(seq_lengths)[:-1]
    positions = lax.axis_index("ctx") * tok_count + jnp.arange(tok_count, dtype=jnp.int32)
    segment = segment_of(positions, seq_ends)
    slot_ids = jnp.arange(seq_lengths.shape[0], dtype=jnp.int32)
    token_adapter_index = jnp.sum(
        jnp.where(segment[:, None] == slot_ids[None, :], seq_adapter[None, :], 0), axis=1
    )
    column_group_index = jnp.arange(rank_cols, dtype=jnp.int32) // RANK
    adapter_mask = (column_group_index[None, :] == token_adapter_index[:, None]).astype(jnp.float32)
    adapter_half_float = adapter_mask.astype(jnp.bfloat16)
    adapter_mask_pair = jnp.concatenate([adapter_mask, adapter_mask], axis=1)
    pair_bf = adapter_mask_pair.astype(jnp.bfloat16)
    matching_first = ((positions >= 1) & (segment_of(positions - 1, seq_ends) == segment)).astype(
        jnp.float32
    )[:, None]
    matching_second = ((positions >= 2) & (segment_of(positions - 2, seq_ends) == segment)).astype(
        jnp.float32
    )[:, None]
    ahead_one = (segment_of(positions + 1, seq_ends) == segment).astype(jnp.float32)[:, None]
    ahead_two = (segment_of(positions + 2, seq_ends) == segment).astype(jnp.float32)[:, None]
    row_pair = (
        lax.all_gather(packed_in, "tensor", axis=1, tiled=True),
        lax.all_gather(packed_cot, "tensor", axis=1, tiled=True),
    )
    input_complete = row_pair[0].astype(jnp.float32)
    cotangent_half_float = row_pair[1]
    cot_full = cotangent_half_float.astype(jnp.float32)
    mixer_f = mixer_gain.astype(jnp.float32)
    ffn_f = ffn_gain.astype(jnp.float32)
    conv_w = conv_taps.astype(jnp.float32)
    in_full, out_full = fetch_mixer(in_weight, out_weight)
    scale_one = rms_scale(input_complete)
    normalized_rows = (input_complete * scale_one * mixer_f).astype(jnp.bfloat16)
    input_rank_rows = (
        product_simple(normalized_rows, input_adapter_shrink).astype(jnp.bfloat16)
        * adapter_half_float
    )
    projected_rows = jnp.einsum(
        "px,sxa->psa", normalized_rows, in_full, preferred_element_type=jnp.float32
    ) + adapter_scale * jnp.einsum(
        "fw,kwo->fko", input_rank_rows, in_expand, preferred_element_type=jnp.float32
    )
    gate_b = projected_rows[:, 0]
    gate_c = projected_rows[:, 1]
    values_x = projected_rows[:, 2]
    mixed = (gate_b * values_x).astype(jnp.bfloat16)
    prior = shifted(mixed[tok_count - 2 :], "ctx", 1)
    extended = jnp.concatenate([prior, mixed], axis=0).astype(jnp.float32)
    conv_out = (
        conv_w[0] * extended[2:]
        + conv_w[1] * extended[1:-1] * matching_first
        + conv_w[2] * extended[:-2] * matching_second
    )
    gated_rows = (gate_c * conv_out).astype(jnp.bfloat16)
    adapter_branch_sum, output_rank_sum = lax.psum(
        (product_simple(gated_rows, out_full), product_simple(gated_rows, out_shrink)), "tensor"
    )
    output_rank_rows = output_rank_sum.astype(jnp.bfloat16) * adapter_half_float
    hidden_state_rows = input_complete + (
        adapter_branch_sum + adapter_scale * product_simple(output_rank_rows, output_adapter_expand)
    )
    scale_two = rms_scale(hidden_state_rows)
    feedforward_input = (hidden_state_rows * scale_two * ffn_f).astype(jnp.bfloat16)
    feedforward_rank_rows = (
        product_simple(feedforward_input, ffn_shrink).astype(jnp.bfloat16) * pair_bf
    )
    ffn_low_split = feedforward_rank_rows.reshape(tok_count, 2, rank_cols)
    gu_full, down_full = fetch_ffn(gateup_weight, down_weight)
    gate_up_output = jnp.einsum(
        "cm,ame->cae", feedforward_input, gu_full, preferred_element_type=jnp.float32
    ) + adapter_scale * jnp.einsum(
        "vmc,mcb->vmb", ffn_low_split, ffn_expand, preferred_element_type=jnp.float32
    )
    gate_pre = gate_up_output[:, 0]
    up_pre = gate_up_output[:, 1]
    activated_rows = (jax.nn.silu(gate_pre) * up_pre).astype(jnp.bfloat16)
    down_weight_slice = lax.psum_scatter(
        product_simple(activated_rows, down_full).astype(jnp.bfloat16),
        "tensor",
        scatter_dimension=1,
        tiled=True,
    ).astype(jnp.float32)
    down_rank_rows_sum = lax.psum(product_simple(activated_rows, down_shrink), "tensor")
    down_rank_rows = down_rank_rows_sum.astype(jnp.bfloat16) * adapter_half_float
    expand_factor_slice = lax.dynamic_slice_in_dim(
        down_adapter_expand, part_index * half_width, half_width, 1
    )
    hidden_column_slice = lax.dynamic_slice_in_dim(
        hidden_state_rows, part_index * half_width, half_width, 1
    )
    packed_output = (
        hidden_column_slice
        + (down_weight_slice + adapter_scale * product_simple(down_rank_rows, expand_factor_slice))
    ).astype(jnp.bfloat16)
    gu_full, down_full = fetch_ffn(gateup_weight, down_weight)
    down_rank_gradient = (
        adapter_scale * product_backward(cotangent_half_float, down_adapter_expand) * adapter_mask
    ).astype(jnp.bfloat16)
    down_adapter_expand_gradient = adapter_scale * product_leading(
        down_rank_rows, cotangent_half_float
    )
    grad_act = product_backward(cotangent_half_float, down_full) + product_backward(
        down_rank_gradient, down_shrink
    )
    down_shrink_grad = product_leading(activated_rows, down_rank_gradient)
    sigmoid_gate = jax.nn.sigmoid(gate_pre)
    grad_gate = grad_act * up_pre * sigmoid_gate * (1.0 + gate_pre * (1.0 - sigmoid_gate))
    grad_up = grad_act * gate_pre * sigmoid_gate
    grad_gu = jnp.stack([grad_gate, grad_up], axis=1).astype(jnp.bfloat16)
    feedforward_expand_gradient = adapter_scale * jnp.einsum(
        "tje,tjf->jef", ffn_low_split, grad_gu, preferred_element_type=jnp.float32
    )
    feedforward_rank_part = adapter_scale * jnp.einsum(
        "tjf,jef->tje", grad_gu, ffn_expand, preferred_element_type=jnp.float32
    ).reshape(tok_count, 2 * rank_cols)
    ffn_in_part = jnp.einsum("tjf,jdf->td", grad_gu, gu_full, preferred_element_type=jnp.float32)
    ffn_in_sum, ffn_low_sum = lax.psum((ffn_in_part, feedforward_rank_part), "tensor")
    grad_ffn_low = (ffn_low_sum * adapter_mask_pair).astype(jnp.bfloat16)
    grad_ffn_in = ffn_in_sum + product_backward(grad_ffn_low, ffn_shrink)
    ffn_shrink_grad = product_leading(feedforward_input, grad_ffn_low)
    grad_hidden = cot_full + norm_back(hidden_state_rows, scale_two, ffn_f, grad_ffn_in)
    in_full, out_full = fetch_mixer(in_weight, out_weight)
    adapter_branch_gradient = grad_hidden.astype(jnp.bfloat16)
    out_rank_gradient = (
        adapter_scale
        * product_backward(adapter_branch_gradient, output_adapter_expand)
        * adapter_mask
    ).astype(jnp.bfloat16)
    output_expand_gradient = adapter_scale * product_leading(
        output_rank_rows, adapter_branch_gradient
    )
    grad_gated = product_backward(adapter_branch_gradient, out_full) + product_backward(
        out_rank_gradient, out_shrink
    )
    out_shrink_grad = product_leading(gated_rows, out_rank_gradient)
    grad_gate_c = grad_gated * conv_out
    grad_conv = grad_gated * gate_c
    ahead = shifted(grad_conv[:2], "ctx", -1)
    trailing = jnp.concatenate([grad_conv, ahead], axis=0)
    grad_mixed = (
        conv_w[0] * grad_conv
        + conv_w[1] * trailing[1:-1] * ahead_one
        + conv_w[2] * trailing[2:] * ahead_two
    )
    grad_proj = jnp.stack([grad_mixed * values_x, grad_gate_c, grad_mixed * gate_b], axis=1).astype(
        jnp.bfloat16
    )
    input_expand_gradient = adapter_scale * jnp.einsum(
        "te,tjc->jec", input_rank_rows, grad_proj, preferred_element_type=jnp.float32
    )
    input_rank_part = adapter_scale * jnp.einsum(
        "tjc,jec->te", grad_proj, in_expand, preferred_element_type=jnp.float32
    )
    normed_part = jnp.einsum("tjc,jdc->td", grad_proj, in_full, preferred_element_type=jnp.float32)
    normed_sum, input_rank_sum = lax.psum((normed_part, input_rank_part), "tensor")
    in_rank_gradient = (input_rank_sum * adapter_mask).astype(jnp.bfloat16)
    grad_normed = normed_sum + product_backward(in_rank_gradient, input_adapter_shrink)
    in_shrink_grad = product_leading(normalized_rows, in_rank_gradient)
    grad_input_full = grad_hidden + norm_back(input_complete, scale_one, mixer_f, grad_normed)
    packed_grad = lax.dynamic_slice_in_dim(grad_input_full, part_index * half_width, half_width, 1)
    output_blocks = jnp.take(
        packed_output.reshape(group_total, block_rows, half_width), inverse_row, axis=0
    )
    grad_blocks = jnp.take(
        packed_grad.reshape(group_total, block_rows, half_width), inverse_row, axis=0
    )
    block_output = lax.all_to_all(
        output_blocks, "dp", split_axis=0, concat_axis=0, tiled=True
    ).reshape(tok_count, half_width)
    input_grad = (
        lax.all_to_all(
            grad_blocks.astype(jnp.bfloat16), "dp", split_axis=0, concat_axis=0, tiled=True
        )
        .astype(grad_blocks.dtype)
        .reshape(tok_count, half_width)
    )
    totals = lax.psum(
        (
            in_shrink_grad,
            input_expand_gradient,
            out_shrink_grad,
            output_expand_gradient,
            ffn_shrink_grad,
            feedforward_expand_gradient,
            down_shrink_grad,
            down_adapter_expand_gradient,
        ),
        ("dp", "ctx"),
    )
    return (
        block_output,
        input_grad,
        totals[0],
        totals[1],
        totals[2],
        totals[3],
        totals[4],
        totals[5],
        totals[6],
        totals[7],
    )


def solution(mesh):
    placed = (
        P(("dp", "ctx"), "tensor"),
        P(("dp", "ctx"), "tensor"),
        P("dp", None),
        P("dp"),
        P("dp"),
        P(),
        P(),
        P(None, "tensor"),
        P(None, "dp", "tensor"),
        P("tensor", "dp"),
        P(None, "dp", "tensor"),
        P("tensor", "dp"),
        P(),
        P(None, None, "tensor"),
        P("tensor", None),
        P(),
        P(),
        P(None, None, "tensor"),
        P("tensor", None),
        P(),
    )
    return jax.shard_map(
        body,
        mesh=mesh,
        in_specs=placed,
        out_specs=(
            P(("dp", "ctx"), "tensor"),
            P(("dp", "ctx"), "tensor"),
            P(),
            P(None, None, "tensor"),
            P("tensor", None),
            P(),
            P(),
            P(None, None, "tensor"),
            P("tensor", None),
            P(),
        ),
        check_vma=False,
    )
```

profile of v0, /device:TPU:0, one launch (start us, length us, event | category | flops | bytes accessed | tf_op | source)
XLA Modules:
  0.0 1380.1 jit_solution(14482190222094816660)
XLA Ops:
  7.2 25.2 %all_to_all.20 = bf16[4,192,1024]{2,1,0:T(8,128)(2,1)} all-to-all(bf16[4,192,1024]{2,1,0:T(8,128)(2,1)} %bitcast.155), channel_id=1, replica_groups=mesh['dp'=4,'ctx'=4,'tensor'=2] {'dp'}, dimensions={0} | all-to-all | bytes 3145728 | tf_op jit(solution)/shard_map/all_to_all | solution.py:95
  32.4 3.6 all-to-all-start.2
  36.1 3.2 gather_fusion.1
  39.3 16.7 %all-to-all-done.2 = bf16[4,192,1024]{2,1,0:T(8,128)(2,1)S(1)} async-done(((bf16[4,192,1024]{2,1,0:T(8,128)(2,1)}), bf16[4,192,1024]{2,1,0:T(8,128)(2,1)S(1)}, u32[]{:S(2)}, u32[]{:S(2)}) %all-to-all-start.2) | async-done | bytes 1572896 | tf_op jit(solution)/shard_map/all_to_all | solution.py:102
  57.9 3.9 broadcast_select_fusion.1
  65.6 42.4 %all-gather.7.cloned.1.call-done = bf16[768,2048]{1,0:T(8,128)(2,1)} async-done(((bf16[768,1024]{1,0:T(8,128)(2,1)}), bf16[768,2048]{1,0:T(8,128)(2,1)}) %all-gather.7.cloned.1.call-update) | async-done | bytes 3145744 | tf_op jit(solution)/shard_map/all_gather | solution.py:133
  108.0 2.7 fusion
  111.9 79.8 %all-gather.9.cloned.1.call-done = bf16[3,2048,1024]{2,1,0:T(8,128)(2,1)} async-done(((bf16[3,512,1024]{2,1,0:T(8,128)(2,1)}), bf16[3,2048,1024]{2,1,0:T(8,128)(2,1)}) %all-gather.9.cloned.1.call-update) | async-done | bytes 12582928 | tf_op jit(solution)/shard_map/all_gather | solution.py:49
  191.7 13.6 fusion.17
  207.3 3.4 collective-permute-start
  212.5 2.9 multiply_convert_fusion.8
  215.4 12.4 all-gather.11.cloned.1.call-done
  227.8 7.4 fusion.72
  237.9 36.9 %all-gather.17.cloned.1.call-done = bf16[768,2048]{1,0:T(8,128)(2,1)} async-done(((bf16[768,1024]{1,0:T(8,128)(2,1)}), bf16[768,2048]{1,0:T(8,128)(2,1)}) %all-gather.17.cloned.1.call-update) | async-done | bytes 3145744 | tf_op jit(solution)/shard_map/all_gather | solution.py:134
  274.8 3.5 fusion.29
  278.3 74.0 %all-gather.15.cloned.1.call-done = bf16[2816,2048]{1,0:T(8,128)(2,1)} async-done(((bf16[2816,512]{1,0:T(8,128)(2,1)}), bf16[2816,2048]{1,0:T(8,128)(2,1)}) %all-gather.15.cloned.1.call-update) | async-done | bytes 11534352 | tf_op jit(solution)/shard_map/all_gather | solution.py:57
  352.3 15.8 %fusion.75 = f32[768,2816]{1,0:T(8,128)} fusion(bf16[768,2048]{1,0:T(8,128)(2,1)} %all-gather.17.cloned.1.call-done, bf16[2816,2048]{1,0:T(8,128)(2,1)} %all-gather.15.cloned.1.call-done), kind=kOutput, calls=%fused_computation.166 | convolution fusion | flops 8858370048 | bytes 23330816 | tf_op jit(solution)/shard_map/dot_general | solution.py:32
  369.5 25.5 %all-reduce.17 = bf16[768,128]{1,0:T(8,128)(2,1)S(1)} all-reduce(f32[768,128]{1,0:T(8,128)} %fusion.73), channel_id=1, replica_groups=mesh['dp'=4,'ctx'=4,'tensor'=2] {'tensor'}, use_global_device_ids=true, to_apply=%region_7.9 | all-reduce | flops 98304 | bytes 589824 | tf_op jit(solution)/shard_map/psum | solution.py:166
  395.0 121.3 %all-reduce.10.cloned.1.call-done = f32[768,2048]{1,0:T(8,128)} async-done(((f32[768,2048]{1,0:T(8,128)}), f32[768,2048]{1,0:T(8,128)}) %all-reduce.10.cloned.1.call-update) | async-done | bytes 6291472 | tf_op jit(solution)/shard_map/psum | solution.py:166
  516.3 4.7 multiply_reduce_fusion.2
  528.2 131.7 %all-gather.13.cloned.1.call-done = bf16[2,2048,2816]{2,1,0:T(8,128)(2,1)} async-done(((bf16[2,512,2816]{2,1,0:T(8,128)(2,1)}), bf16[2,2048,2816]{2,1,0:T(8,128)(2,1)}) %all-gather.13.cloned.1.call-update) | async-done | bytes 23068688 | tf_op jit(solution)/shard_map/all_gather | solution.py:56
  659.9 23.8 %fusion.15 = f32[768,2,2816]{2,0,1:T(8,128)S(1)} fusion(bf16[2,2048,2816]{2,1,0:T(8,128)(2,1)} %all-gather.13.cloned.1.call-done, bf16[768,2048]{1,0:T(8,128)(2,1)} %copy-done.11), kind=kOutput, calls=%fused_computation.57 | convolution fusion | flops 17716740096 | bytes 43515904 | tf_op jit(solution)/shard_map/cm,ame->cae/dot_general | solution.py:180
  683.6 9.4 bitcast_add_fusion
  693.0 13.5 fusion.2
  706.6 5.8 fusion.24
  713.6 25.4 %convolution_bitcast_fusion.1 = f32[768,2048]{1,0:T(8,128)} fusion(bf16[2,2048,2816]{2,1,0:T(8,128)(2,1)} %all-gather.13.cloned.1.call-done, bf16[768,1,2816]{2,0,1:T(8,128)(2,1)} %get-tuple-element.53, bf16[768,1,2816]{2,0,1:T(8,128)(2,1)} %copy-done.65), kind=kOutput, calls=%fused_computation.31 | convolution fusion | flops 17721065472 | bytes 38010880 | tf_op jit(solution)/shard_map/tjf,jdf->td/dot_general | solution.py:227
  739.0 14.4 %convolution_convert_fusion = bf16[768,2048]{1,0:T(8,128)(2,1)} fusion(bf16[768,2816]{1,0:T(8,128)(2,1)} %get-tuple-element.54, bf16[2816,2048]{1,0:T(8,128)(2,1)} %all-gather.15.cloned.1.call-done), kind=kOutput, calls=%fused_computation.32 | convolution fusion | flops 8859942912 | bytes 19005440 | tf_op jit(solution)/shard_map/dot_general | solution.py:28
  753.6 156.1 %all-reduce.16.cloned.1.call-done = (f32[768,2048]{1,0:T(8,128)}, f32[768,256]{1,0:T(8,128)}) async-done(((f32[768,2048]{1,0:T(8,128)}, f32[768,256]{1,0:T(8,128)}), (f32[768,2048]{1,0:T(8,128)}, f32[768,256]{1,0:T(8,128)})) %all-reduce.16.cloned.1.call-update) | async-done | bytes 7077904 | tf_op jit(solution)/shard_map/psum | solution.py:228
  909.7 6.5 multiply_reduce_fusion.1
  922.4 3.5 fusion.61
  930.6 4.2 collective-permute-done.1
  934.9 3.4 fusion.21
  940.3 14.7 %convolution_bitcast_fusion = f32[768,2048]{1,0:T(8,128)} fusion(bf16[3,2048,1024]{2,1,0:T(8,128)(2,1)} %all-gather.9.cloned.1.call-done, bf16[768,1,1024]{2,0,1:T(8,128)(2,1)S(1)} %fusion.23, bf16[768,1,1024]{2,0,1:T(8,128)(2,1)S(1)} %get-tuple-element.57, bf16[768,1,1024]{2,0,1:T(8,128)(2,1)S(1)} %get-tuple-element.48), kind=kOutput, calls=%fused_computation.30 | convolution fusion | flops 9668395008 | bytes 23592960 | tf_op jit(solution)/shard_map/tjc,jdc->td/dot_general | solution.py:265
  955.3 3.7 fusion.74
  959.1 4.8 fusion.77
  963.9 6.9 convolution_multiply_fusion
  978.8 41.3 %all-reduce.18 = (bf16[768,128]{1,0:T(8,128)(2,1)S(1)}, bf16[768,128]{1,0:T(8,128)(2,1)S(1)}) all-reduce(f32[768,128]{1,0:T(8,128)S(1)} %fusion.74, f32[768,128]{1,0:T(8,128)S(1)} %fusion.27), channel_id=1, replica_groups=mesh['dp'=4,'ctx'=4,'tensor'=2] {'tensor'}, use_global_device_ids=true, to_apply=%region_10.12 | all-reduce | flops 196608 | bytes 1179648 | tf_op jit(solution)/shard_map/psum | solution.py:194
  1020.1 3.7 convolution_multiply_fusion.1
  1026.4 2.6 multiply_bitcast_fusion
  1030.1 3.0 add_convert_fusion
  1035.0 92.8 %all-reduce.12.cloned.1.call-done = f32[768,2048]{1,0:T(8,128)} async-done(((f32[768,2048]{1,0:T(8,128)}), f32[768,2048]{1,0:T(8,128)}) %all-reduce.12.cloned.1.call-update) | async-done | bytes 6291472 | tf_op jit(solution)/shard_map/psum | solution.py:266
  1127.8 4.9 multiply_reduce_fusion
  1137.1 4.1 select_convert_fusion
  1141.1 39.8 %all_to_all.21 = bf16[4,192,1024]{2,1,0:T(8,128)(2,1)S(1)} all-to-all(bf16[4,192,1024]{2,1,0:T(8,128)(2,1)S(1)} %get-tuple-element.67), channel_id=1, replica_groups=mesh['dp'=4,'ctx'=4,'tensor'=2] {'dp'}, dimensions={0} | all-to-all | bytes 3145728 | tf_op jit(solution)/shard_map/all_to_all | solution.py:278
  1180.9 4.4 all-to-all-start.3
  1185.3 170.9 %all-reduce.14.cloned.1.call-done = (f32[2048,128]{1,0:T(8,128)}, f32[3,128,1024]{1,2,0:T(8,128)}, f32[1024,128]{1,0:T(8,128)}, f32[128,2048]{1,0:T(8,128)}, f32...) async-done(((f32[2048,128]{1,0:T(8,128)}, f32[3,128,1024]{1,2,0:T(8,128)}, f32[1024,128]{1,0:T(8,128)}, ...) | async-done | bytes 11665424 | tf_op jit(solution)/shard_map/psum | solution.py:288
  1356.2 3.0 copy.41
  1359.2 3.6 bitcast_convert_fusion
  (234 shorter events, 63.7 us)
Async XLA Ops:
  7.2 676.5 %copy-start = (bf16[2,128,2816]{2,1,0:T(8,128)(2,1)S(1)}, bf16[2,128,2816]{2,1,0:T(8,128)(2,1)}, u32[]{:S(2)}) copy-start(bf16[2,128,2816]{2,1,0:T(8,128)(2,1)} %param.39) | copy-start | bytes 4325380
  7.2 28.9 %copy-start.63 = (s32[1,4]{1,0:T(1,128)S(1)}, s32[1,4]{1,0:T(1,128)}, u32[]{:S(2)}) copy-start(s32[1,4]{1,0:T(1,128)} %param.24) | copy-start | bytes 52
  32.4 23.6 %all-to-all-start.2 = ((bf16[4,192,1024]{2,1,0:T(8,128)(2,1)}), bf16[4,192,1024]{2,1,0:T(8,128)(2,1)S(1)}, u32[]{:S(2)}, u32[]{:S(2)}) async-start(bf16[4,192,1024]{2,1,0:T(8,128)(2,1)} %bitcast.156), calls=%async_computation.3 | async-start | bytes 3145728 | tf_op jit(solution)/shard_map/all_to_all | solution.py:102
  36.0 72.0 %all-gather.7.cloned.1.call-start = ((), (), s32[]{:S(2)}) async-start(), calls=%async_computation.5 | async-start | bytes 4718592 | tf_op jit(solution)/shard_map/all_gather | solution.py:133
  61.8 130.0 %all-gather.9.cloned.1.call-start = ((), (), s32[]{:S(2)}) async-start(), calls=%async_computation.6 | async-start | bytes 15728640 | tf_op jit(solution)/shard_map/all_gather | solution.py:49
  62.6 165.3 %all-gather.11.cloned.1.call-start = ((), (), s32[]{:S(2)}) async-start(), calls=%async_computation.7 | async-start | bytes 5242880 | tf_op jit(solution)/shard_map/all_gather | solution.py:50
  63.3 211.5 %all-gather.17.cloned.1.call-start = ((), (), s32[]{:S(2)}) async-start(), calls=%async_computation.12 | async-start | bytes 4718592 | tf_op jit(solution)/shard_map/all_gather | solution.py:134
  63.9 46.9 %copy-start.38 = (bf16[2048,128]{1,0:T(8,128)(2,1)S(1)}, bf16[2048,128]{1,0:T(8,128)(2,1)}, u32[]{:S(2)}) copy-start(bf16[2048,128]{1,0:T(8,128)(2,1)} %param.34) | copy-start | bytes 1572868
  63.9 288.5 %all-gather.15.cloned.1.call-start = ((), (), s32[]{:S(2)}) async-start(), calls=%async_computation.10 | async-start | bytes 14417920 | tf_op jit(solution)/shard_map/all_gather | solution.py:57
  64.5 451.9 %all-reduce.10.cloned.1.call-start = ((), (), s32[]{:S(2)}) async-start(), calls=%async_computation.8 | async-start | bytes 12582912 | tf_op jit(solution)/shard_map/psum | solution.py:166
  64.5 127.2 %copy-start.54 = (f32[2048]{0:T(1024)}, f32[2048]{0:T(1024)S(1)}, u32[]{:S(2)}) copy-start(f32[2048]{0:T(1024)S(1)} %convert_element_type.128) | copy-start | bytes 24580
  110.9 80.9 %copy-start.46 = (f32[768]{0:T(1024)}, f32[768]{0:T(1024)S(1)}, u32[]{:S(2)}) copy-start(f32[768]{0:T(1024)S(1)} %add_rsqrt_fusion.1) | copy-start | bytes 9220
  111.9 93.4 %copy-start.41 = (bf16[768,128,1]{1,0,2:T(8,128)(2,1)}, bf16[768,128,1]{1,0,2:T(8,128)(2,1)S(1)}, u32[]{:S(2)}) copy-start(bf16[768,128,1]{1,0,2:T(8,128)(2,1)S(1)} %fusion.32) | copy-start | bytes 589828
  111.9 93.4 %copy-start.28 = (bf16[3,128,1024]{2,1,0:T(8,128)(2,1)S(1)}, bf16[3,128,1024]{2,1,0:T(8,128)(2,1)}, u32[]{:S(2)}) copy-start(bf16[3,128,1024]{2,1,0:T(8,128)(2,1)} %param.35) | copy-start | bytes 2359300
  206.8 5.8 copy-start.3
  207.3 4.7 collective-permute-start
  215.4 152.8 %copy-start.7 = (bf16[768,1024]{1,0:T(8,128)(2,1)}, bf16[768,1024]{1,0:T(8,128)(2,1)S(1)}, u32[]{:S(2)}) copy-start(bf16[768,1024]{1,0:T(8,128)(2,1)S(1)} %get-tuple-element.50) | copy-start | bytes 4718596
  235.2 39.5 %copy-start.44 = (bf16[128,2048]{1,0:T(8,128)(2,1)S(1)}, bf16[128,2048]{1,0:T(8,128)(2,1)}, u32[]{:S(2)}) copy-start(bf16[128,2048]{1,0:T(8,128)(2,1)} %param.41) | copy-start | bytes 1572868
  235.2 424.6 %all-gather.13.cloned.1.call-start = ((), (), s32[]{:S(2)}) async-start(), calls=%async_computation.9 | async-start | bytes 28835840 | tf_op jit(solution)/shard_map/all_gather | solution.py:56
  236.0 673.7 %all-reduce.16.cloned.1.call-start = ((), (), s32[]{:S(2)}) async-start(), calls=%async_computation.15 | async-start | bytes 14155776 | tf_op jit(solution)/shard_map/psum | solution.py:228
  352.3 15.8 %copy-start.32 = (bf16[1024,128]{1,0:T(8,128)(2,1)S(1)}, bf16[1024,128]{1,0:T(8,128)(2,1)}, u32[]{:S(2)}) copy-start(bf16[1024,128]{1,0:T(8,128)(2,1)} %param.36) | copy-start | bytes 786436
  368.2 148.1 %copy-start.14 = (bf16[128,2048]{1,0:T(8,128)(2,1)S(1)}, bf16[128,2048]{1,0:T(8,128)(2,1)}, u32[]{:S(2)}) copy-start(bf16[128,2048]{1,0:T(8,128)(2,1)} %param.37) | copy-start | bytes 1572868
  395.0 126.0 %copy-start.16 = (bf16[768,128]{1,0:T(8,128)(2,1)}, bf16[768,128]{1,0:T(8,128)(2,1)S(1)}, u32[]{:S(2)}) copy-start(bf16[768,128]{1,0:T(8,128)(2,1)S(1)} %all-reduce.17) | copy-start | bytes 589828
  706.6 5.8 copy-start.65
  739.0 290.9 %reduce-scatter.2.cloned.1.call-start = ((), (), s32[]{:S(2)}) async-start(), calls=%async_computation.11 | async-start | bytes 4718592 | tf_op jit(solution)/shard_map/reduce_scatter | solution.py:188
  753.5 156.2 %copy-start.26 = (f32[768,128]{1,0:T(8,128)S(1)}, f32[768,128]{1,0:T(8,128)}, u32[]{:S(2)}) copy-start(f32[768,128]{1,0:T(8,128)} %compare_convert_fusion) | copy-start | bytes 1179652
  753.5 156.2 %copy-start.31 = (bf16[2048,256]{1,0:T(8,128)(2,1)S(1)}, bf16[2048,256]{1,0:T(8,128)(2,1)}, u32[]{:S(2)}) copy-start(bf16[2048,256]{1,0:T(8,128)(2,1)} %param.38) | copy-start | bytes 3145732
  753.5 374.3 %all-reduce.12.cloned.1.call-start = ((), (), s32[]{:S(2)}) async-start(), calls=%async_computation.13 | async-start | bytes 12582912 | tf_op jit(solution)/shard_map/psum | solution.py:266
  909.7 6.6 slice-start
  909.7 6.7 slice-start.1
  909.7 7.6 copy-start.9
  919.2 7.3 slice-start.2
  927.7 7.2 copy-start.49
  927.7 7.2 copy-start.51
  927.7 7.2 copy-start.53
  927.7 7.2 copy-start.57
  927.7 7.2 copy-start.58
  929.3 5.5 collective-permute-start.1
  955.0 401.1 %all-reduce.14.cloned.1.call-start = ((), (), s32[]{:S(2)}) async-start(), calls=%async_computation.14 | async-start | bytes 23330816 | tf_op jit(solution)/shard_map/psum | solution.py:288
  959.1 15.6 %slice-start.5 = ((s8[6291456]{0:T(1024)(128)(4,1)}), s8[4194304]{0:T(1024)(128)(4,1)S(1)}, s32[]{:S(2)}) async-start(s8[6291456]{0:T(1024)(128)(4,1)} %bitcast.146), calls=%async_computation.21 | async-start | bytes 8388608
  963.9 7.0 copy-start.8
  963.9 8.4 copy-start.12
  963.9 8.4 copy-start.37
  963.9 10.8 slice-start.6
  978.8 45.0 %copy-start.47 = (f32[768]{0:T(1024)S(1)}, f32[768]{0:T(1024)}, u32[]{:S(2)}) copy-start(f32[768]{0:T(1024)} %copy-done.46) | copy-start | bytes 9220
  978.8 45.0 %copy-start.55 = (f32[2048]{0:T(1024)S(1)}, f32[2048]{0:T(1024)}, u32[]{:S(2)}) copy-start(f32[2048]{0:T(1024)} %copy-done.54) | copy-start | bytes 24580
  1033.2 94.6 %copy-start.39 = (bf16[2048,128]{1,0:T(8,128)(2,1)S(1)}, bf16[2048,128]{1,0:T(8,128)(2,1)}, u32[]{:S(2)}) copy-start(bf16[2048,128]{1,0:T(8,128)(2,1)} %param.34) | copy-start | bytes 1572868
  1180.9 178.3 %all-to-all-start.3 = ((bf16[4,192,1024]{2,1,0:T(8,128)(2,1)}), bf16[4,192,1024]{2,1,0:T(8,128)(2,1)}, u32[]{:S(2)}, u32[]{:S(2)}) async-start(bf16[4,192,1024]{2,1,0:T(8,128)(2,1)} %get-tuple-element.66), calls=%async_computation.4 | async-start | bytes 3145728 | tf_op jit(solution)/shard_map/all_to_all | solution.py:282
  (40 other events, 115.2 us)
Sparse Core Ops, SparseCore 0:
  61.9 46.0 all-gather.6
  109.6 82.0 all-gather.8
  193.3 34.4 all-gather.10
  229.8 44.9 all-gather.16
  276.2 76.1 all-gather.14
  354.6 161.6 all-reduce.9
  518.0 141.8 all-gather.12
  739.1 170.5 all-reduce.15
  911.9 43.3 reduce-scatter.1
  957.7 170.0 all-reduce.11
  1133.8 222.3 all-reduce.13
where the time goes:
time: 1390 us; the launch traced here: 1380 us
  waiting for transfers between devices  944 us (68%)
  matrix products  208 us (15%)
  blocking collectives  132 us (9%)
  local copies, waits for them, and re-layouts  36.4 us (3%)
  other arithmetic  31.6 us (2%)
  between operations  15.3 us (1%)
    psum x1, waiting for transfers between devices, body(): lax.psum((in_shrink_grad, input_expand_gradient, out_shrink_grad, output_...  171 us
    psum x1, waiting for transfers between devices, body(): lax.psum((ffn_in_part, feedforward_rank_part), 'tensor')  156 us
    all_gather x1, waiting for transfers between devices, fetch_ffn(): lax.all_gather(gateup_weight, 'dp', axis=1, tiled=True)  132 us
    psum x1, waiting for transfers between devices, body(): lax.psum((product_simple(gated_rows, out_full), product_simple(gated_rows...  121 us
    psum x1, waiting for transfers between devices, body(): lax.psum((normed_part, input_rank_part), 'tensor')  92.8 us
    all_gather x1, waiting for transfers between devices, fetch_mixer(): lax.all_gather(in_weight, 'dp', axis=1, tiled=True)  79.8 us
    all_gather x1, waiting for transfers between devices, fetch_ffn(): lax.all_gather(down_weight, 'dp', axis=1, tiled=True)  74 us
    dot_general x8, matrix products, product_backward(): lax.dot_general(left, right, (((1,), (1,)), ((), ())), preferred_element_...  49.3 us
  transfers between devices with their start and end apart: 15, of which 13 were waited for; matrix products, arithmetic and copies ran while one was open for 12% of the time, Pallas kernels for 0%

commit v1 on v0

--- a/solution.py
+++ b/solution.py
@@ -286,17 +286,20 @@
         .reshape(tok_count, half_width)
     )
     totals = lax.psum(
-        (
-            in_shrink_grad,
-            input_expand_gradient,
-            out_shrink_grad,
-            output_expand_gradient,
-            ffn_shrink_grad,
-            feedforward_expand_gradient,
-            down_shrink_grad,
-            down_adapter_expand_gradient,
+        lax.psum(
+            (
+                in_shrink_grad,
+                input_expand_gradient,
+                out_shrink_grad,
+                output_expand_gradient,
+                ffn_shrink_grad,
+                feedforward_expand_gradient,
+                down_shrink_grad,
+                down_adapter_expand_gradient,
+            ),
+            "ctx",
         ),
-        ("dp", "ctx"),
+        "dp",
     )
     return (
         block_output,

time: 1390 us -> 1850 us (1.33)
  waiting for transfers between devices: 944 us -> 1430 us
  blocking collectives: 132 us -> 111 us
    psum x1, waiting for transfers between devices: 171 us -> 371 us  [body(): lax.psum((in_shrink_grad, input_expand_gradient, out_shrink_grad, output_...]
    psum x0 -> x1, waiting for transfers between devices: none -> 147 us  [body(): lax.psum(lax.psum((in_shrink_grad, input_expand_gradient, out_shrink_grad...]
    psum x1, waiting for transfers between devices: 92.8 us -> 151 us  [body(): lax.psum((normed_part, input_rank_part), 'tensor')]
    reduce_scatter x1, waiting for transfers between devices: 0.02 us -> 44.2 us  [body(): lax.psum_scatter(product_simple(activated_rows, down_full).astype(jnp.bfl...]
    all_to_all x1, waiting for transfers between devices: 0.01 us -> 37.4 us  [body(): lax.all_to_all(grad_blocks.astype(jnp.bfloat16), 'dp', split_axis=0, conc...]
    psum x1, blocking collectives: 41.3 us -> 20.6 us  [body(): lax.psum(product_simple(activated_rows, down_shrink), 'tensor')]
  transfers between devices with their start and end apart: 15 -> 16, of which waited for: 13 -> 16; matrix products, arithmetic and copies ran while one was open for 12% -> 7% of each run, Pallas kernels for 0% -> 0%
where the time goes in v1:
time: 1850 us; the launch traced here: 1840 us
  waiting for transfers between devices  1430 us (77%)
  matrix products  208 us (11%)
  blocking collectives  111 us (6%)
  local copies, waits for them, and re-layouts  35.4 us (2%)
  other arithmetic  31.6 us (2%)
    psum x1, waiting for transfers between devices, body(): lax.psum((in_shrink_grad, input_expand_gradient, out_shrink_grad, output_...  371 us
    psum x1, waiting for transfers between devices, body(): lax.psum((ffn_in_part, feedforward_rank_part), 'tensor')  155 us
    psum x1, waiting for transfers between devices, body(): lax.psum((normed_part, input_rank_part), 'tensor')  151 us
    psum x1, waiting for transfers between devices, body(): lax.psum(lax.psum((in_shrink_grad, input_expand_gradient, out_shrink_grad...  147 us
    all_gather x1, waiting for transfers between devices, fetch_ffn(): lax.all_gather(gateup_weight, 'dp', axis=1, tiled=True)  132 us
    psum x1, waiting for transfers between devices, body(): lax.psum((product_simple(gated_rows, out_full), product_simple(gated_rows...  121 us
    all_gather x1, waiting for transfers between devices, fetch_mixer(): lax.all_gather(in_weight, 'dp', axis=1, tiled=True)  79.8 us
    all_gather x1, waiting for transfers between devices, fetch_ffn(): lax.all_gather(down_weight, 'dp', axis=1, tiled=True)  74 us
  transfers between devices with their start and end apart: 16, of which 16 were waited for; matrix products, arithmetic and copies ran while one was open for 7% of the time, Pallas kernels for 0%

profile of v1, /device:TPU:0, one launch (start us, length us, event | category | flops | bytes accessed | tf_op | source)
XLA Modules:
  0.0 1842.9 jit_solution(12957811879445070561)
XLA Ops:
  7.2 25.2 %all_to_all.20 = bf16[4,192,1024]{2,1,0:T(8,128)(2,1)} all-to-all(bf16[4,192,1024]{2,1,0:T(8,128)(2,1)} %bitcast.153), channel_id=1, replica_groups=mesh['dp'=4,'ctx'=4,'tensor'=2] {'dp'}, dimensions={0} | all-to-all | bytes 3145728 | tf_op jit(solution)/shard_map/all_to_all | solution.py:95
  32.4 3.6 all-to-all-start.2
  36.1 3.2 gather_fusion.1
  39.3 16.7 all-to-all-done.2
  57.9 3.9 broadcast_select_fusion.1
  65.6 42.4 %all-gather.7.cloned.1.call-done = bf16[768,2048]{1,0:T(8,128)(2,1)} async-done(((bf16[768,1024]{1,0:T(8,128)(2,1)}), bf16[768,2048]{1,0:T(8,128)(2,1)}) %all-gather.7.cloned.1.call-update) | async-done | bytes 3145744 | tf_op jit(solution)/shard_map/all_gather | solution.py:133
  111.9 79.8 %all-gather.9.cloned.1.call-done = bf16[3,2048,1024]{2,1,0:T(8,128)(2,1)} async-done(((bf16[3,512,1024]{2,1,0:T(8,128)(2,1)}), bf16[3,2048,1024]{2,1,0:T(8,128)(2,1)}) %all-gather.9.cloned.1.call-update) | async-done | bytes 12582928 | tf_op jit(solution)/shard_map/all_gather | solution.py:49
  191.7 13.6 fusion.17
  207.3 3.4 collective-permute-start
  215.4 12.4 all-gather.11.cloned.1.call-done
  227.8 7.4 fusion.72
  237.9 36.9 %all-gather.17.cloned.1.call-done = bf16[768,2048]{1,0:T(8,128)(2,1)} async-done(((bf16[768,1024]{1,0:T(8,128)(2,1)}), bf16[768,2048]{1,0:T(8,128)(2,1)}) %all-gather.17.cloned.1.call-update) | async-done | bytes 3145744 | tf_op jit(solution)/shard_map/all_gather | solution.py:134
  274.8 3.6 fusion.29
  278.3 74.0 %all-gather.15.cloned.1.call-done = bf16[2816,2048]{1,0:T(8,128)(2,1)} async-done(((bf16[2816,512]{1,0:T(8,128)(2,1)}), bf16[2816,2048]{1,0:T(8,128)(2,1)}) %all-gather.15.cloned.1.call-update) | async-done | bytes 11534352 | tf_op jit(solution)/shard_map/all_gather | solution.py:57
  352.3 15.8 fusion.75
  369.5 25.5 %all-reduce.21 = bf16[768,128]{1,0:T(8,128)(2,1)S(1)} all-reduce(f32[768,128]{1,0:T(8,128)} %fusion.73), channel_id=1, replica_groups=mesh['dp'=4,'ctx'=4,'tensor'=2] {'tensor'}, use_global_device_ids=true, to_apply=%region_7.9 | all-reduce | flops 98304 | bytes 589824 | tf_op jit(solution)/shard_map/psum | solution.py:166
  395.1 121.3 %all-reduce.12.cloned.1.call-done = f32[768,2048]{1,0:T(8,128)} async-done(((f32[768,2048]{1,0:T(8,128)}), f32[768,2048]{1,0:T(8,128)}) %all-reduce.12.cloned.1.call-update) | async-done | bytes 6291472 | tf_op jit(solution)/shard_map/psum | solution.py:166
  516.3 4.7 multiply_reduce_fusion.2
  528.2 131.7 %all-gather.13.cloned.1.call-done = bf16[2,2048,2816]{2,1,0:T(8,128)(2,1)} async-done(((bf16[2,512,2816]{2,1,0:T(8,128)(2,1)}), bf16[2,2048,2816]{2,1,0:T(8,128)(2,1)}) %all-gather.13.cloned.1.call-update) | async-done | bytes 23068688 | tf_op jit(solution)/shard_map/all_gather | solution.py:56
  659.9 23.8 %fusion.15 = f32[768,2,2816]{2,0,1:T(8,128)S(1)} fusion(bf16[2,2048,2816]{2,1,0:T(8,128)(2,1)} %all-gather.13.cloned.1.call-done, bf16[768,2048]{1,0:T(8,128)(2,1)} %copy-done.12), kind=kOutput, calls=%fused_computation.57 | convolution fusion | flops 17716740096 | bytes 43515904 | tf_op jit(solution)/shard_map/cm,ame->cae/dot_general | solution.py:180
  683.6 9.4 bitcast_add_fusion
  693.0 13.4 fusion.2
  706.4 5.8 fusion.24
  713.4 25.4 %convolution_bitcast_fusion.1 = f32[768,2048]{1,0:T(8,128)} fusion(bf16[2,2048,2816]{2,1,0:T(8,128)(2,1)} %all-gather.13.cloned.1.call-done, bf16[768,1,2816]{2,0,1:T(8,128)(2,1)} %get-tuple-element.61, bf16[768,1,2816]{2,0,1:T(8,128)(2,1)} %copy-done.62), kind=kOutput, calls=%fused_computation.31 | convolution fusion | flops 17721065472 | bytes 38010880 | tf_op jit(solution)/shard_map/tjf,jdf->td/dot_general | solution.py:227
  740.0 3.6 fusion.74
  743.7 5.7 fusion.77
  749.4 5.4 convolution_multiply_fusion
  754.8 154.7 %all-reduce.20.cloned.1.call-done = (f32[768,2048]{1,0:T(8,128)}, f32[768,256]{1,0:T(8,128)}) async-done(((f32[768,2048]{1,0:T(8,128)}, f32[768,256]{1,0:T(8,128)}), (f32[768,2048]{1,0:T(8,128)}, f32[768,256]{1,0:T(8,128)})) %all-reduce.20.cloned.1.call-update) | async-done | bytes 7077904 | tf_op jit(solution)/shard_map/psum | solution.py:228
  909.6 4.6 fusion.66
  914.5 4.7 multiply_reduce_fusion.1
  926.5 3.5 fusion.61
  939.0 3.4 fusion.21
  947.7 20.6 %all-reduce.22 = (bf16[768,128]{1,0:T(8,128)(2,1)S(1)}, bf16[768,128]{1,0:T(8,128)(2,1)S(1)}) all-reduce(f32[768,128]{1,0:T(8,128)S(1)} %fusion.74, f32[768,128]{1,0:T(8,128)S(1)} %fusion.27), channel_id=1, replica_groups=mesh['dp'=4,'ctx'=4,'tensor'=2] {'tensor'}, use_global_device_ids=true, to_apply=%region_10.12 | all-reduce | flops 196608 | bytes 1179648 | tf_op jit(solution)/shard_map/psum | solution.py:194
  968.3 4.4 fusion.63
  974.4 14.3 convolution_convert_fusion
  988.8 15.8 convolution_bitcast_fusion
  1004.8 371.2 %all-reduce.16.cloned.1.call-done = (f32[2048,128]{1,0:T(8,128)}, f32[3,128,1024]{1,2,0:T(8,128)}, f32[1024,128]{1,0:T(8,128)}, f32[128,2048]{1,0:T(8,128)}, f32...) async-done(((f32[2048,128]{1,0:T(8,128)}, f32[3,128,1024]{1,2,0:T(8,128)}, f32[1024,128]{1,0:T(8,128)}, ...) | async-done | bytes 11665424 | tf_op jit(solution)/shard_map/psum | solution.py:289
  1376.8 44.2 %reduce-scatter.2.cloned.1.call-done = bf16[768,1024]{1,0:T(8,128)(2,1)} async-done(((bf16[768,2048]{1,0:T(8,128)(2,1)}), bf16[768,1024]{1,0:T(8,128)(2,1)}) %reduce-scatter.2.cloned.1.call-update) | async-done | bytes 1572880 | tf_op jit(solution)/shard_map/reduce_scatter | solution.py:188
  1421.0 3.0 add_convert_fusion
  1425.9 150.8 %all-reduce.14.cloned.1.call-done = f32[768,2048]{1,0:T(8,128)} async-done(((f32[768,2048]{1,0:T(8,128)}), f32[768,2048]{1,0:T(8,128)}) %all-reduce.14.cloned.1.call-update) | async-done | bytes 6291472 | tf_op jit(solution)/shard_map/psum | solution.py:266
  1576.7 4.9 multiply_reduce_fusion
  1586.0 4.4 select_convert_fusion
  1590.4 39.9 %all_to_all.21 = bf16[4,192,1024]{2,1,0:T(8,128)(2,1)S(1)} all-to-all(bf16[4,192,1024]{2,1,0:T(8,128)(2,1)S(1)} %get-tuple-element.75), channel_id=1, replica_groups=mesh['dp'=4,'ctx'=4,'tensor'=2] {'dp'}, dimensions={0} | all-to-all | bytes 3145728 | tf_op jit(solution)/shard_map/all_to_all | solution.py:278
  1630.3 4.4 all-to-all-start.3
  1634.7 37.4 %all-to-all-done.3 = bf16[4,192,1024]{2,1,0:T(8,128)(2,1)} async-done(((bf16[4,192,1024]{2,1,0:T(8,128)(2,1)}), bf16[4,192,1024]{2,1,0:T(8,128)(2,1)}, u32[]{:S(2)}, u32[]{:S(2)}) %all-to-all-start.3) | async-done | bytes 1572896 | tf_op jit(solution)/shard_map/all_to_all | solution.py:282
  1672.1 3.5 bitcast_convert_fusion
  1675.5 146.6 %all-reduce.18.cloned.1.call-done = (f32[2048,128]{1,0:T(8,128)}, f32[3,128,1024]{1,2,0:T(8,128)}, f32[1024,128]{1,0:T(8,128)}, f32[128,2048]{1,0:T(8,128)}, f32...) async-done(((f32[2048,128]{1,0:T(8,128)}, f32[3,128,1024]{1,2,0:T(8,128)}, f32[1024,128]{1,0:T(8,128)}, ...) | async-done | bytes 11665424 | tf_op jit(solution)/shard_map/psum | solution.py:288
  1822.2 3.1 copy.41
  (231 shorter events, 70.0 us)
Async XLA Ops:
  7.2 676.5 %copy-start = (bf16[2,128,2816]{2,1,0:T(8,128)(2,1)S(1)}, bf16[2,128,2816]{2,1,0:T(8,128)(2,1)}, u32[]{:S(2)}) copy-start(bf16[2,128,2816]{2,1,0:T(8,128)(2,1)} %param.39) | copy-start | bytes 4325380
  7.2 28.9 %copy-start.60 = (s32[1,4]{1,0:T(1,128)S(1)}, s32[1,4]{1,0:T(1,128)}, u32[]{:S(2)}) copy-start(s32[1,4]{1,0:T(1,128)} %param.24) | copy-start | bytes 52
  32.4 23.6 %all-to-all-start.2 = ((bf16[4,192,1024]{2,1,0:T(8,128)(2,1)}), bf16[4,192,1024]{2,1,0:T(8,128)(2,1)S(1)}, u32[]{:S(2)}, u32[]{:S(2)}) async-start(bf16[4,192,1024]{2,1,0:T(8,128)(2,1)} %bitcast.154), calls=%async_computation.3 | async-start | bytes 3145728 | tf_op jit(solution)/shard_map/all_to_all | solution.py:102
  36.0 72.0 %all-gather.7.cloned.1.call-start = ((), (), s32[]{:S(2)}) async-start(), calls=%async_computation.5 | async-start | bytes 4718592 | tf_op jit(solution)/shard_map/all_gather | solution.py:133
  61.8 130.0 %all-gather.9.cloned.1.call-start = ((), (), s32[]{:S(2)}) async-start(), calls=%async_computation.6 | async-start | bytes 15728640 | tf_op jit(solution)/shard_map/all_gather | solution.py:49
  62.6 165.3 %all-gather.11.cloned.1.call-start = ((), (), s32[]{:S(2)}) async-start(), calls=%async_computation.7 | async-start | bytes 5242880 | tf_op jit(solution)/shard_map/all_gather | solution.py:50
  63.3 211.5 %all-gather.17.cloned.1.call-start = ((), (), s32[]{:S(2)}) async-start(), calls=%async_computation.12 | async-start | bytes 4718592 | tf_op jit(solution)/shard_map/all_gather | solution.py:134
  63.9 46.9 %copy-start.35 = (bf16[2048,128]{1,0:T(8,128)(2,1)S(1)}, bf16[2048,128]{1,0:T(8,128)(2,1)}, u32[]{:S(2)}) copy-start(bf16[2048,128]{1,0:T(8,128)(2,1)} %param.34) | copy-start | bytes 1572868
  63.9 288.5 %all-gather.15.cloned.1.call-start = ((), (), s32[]{:S(2)}) async-start(), calls=%async_computation.10 | async-start | bytes 14417920 | tf_op jit(solution)/shard_map/all_gather | solution.py:57
  64.5 451.8 %all-reduce.12.cloned.1.call-start = ((), (), s32[]{:S(2)}) async-start(), calls=%async_computation.8 | async-start | bytes 12582912 | tf_op jit(solution)/shard_map/psum | solution.py:166
  64.5 127.2 %copy-start.51 = (f32[2048]{0:T(1024)}, f32[2048]{0:T(1024)S(1)}, u32[]{:S(2)}) copy-start(f32[2048]{0:T(1024)S(1)} %convert_element_type.128) | copy-start | bytes 24580
  110.9 80.9 %copy-start.43 = (f32[768]{0:T(1024)}, f32[768]{0:T(1024)S(1)}, u32[]{:S(2)}) copy-start(f32[768]{0:T(1024)S(1)} %add_rsqrt_fusion.1) | copy-start | bytes 9220
  111.9 93.4 %copy-start.38 = (bf16[768,128,1]{1,0,2:T(8,128)(2,1)}, bf16[768,128,1]{1,0,2:T(8,128)(2,1)S(1)}, u32[]{:S(2)}) copy-start(bf16[768,128,1]{1,0,2:T(8,128)(2,1)S(1)} %fusion.32) | copy-start | bytes 589828
  111.9 93.4 %copy-start.24 = (bf16[3,128,1024]{2,1,0:T(8,128)(2,1)S(1)}, bf16[3,128,1024]{2,1,0:T(8,128)(2,1)}, u32[]{:S(2)}) copy-start(bf16[3,128,1024]{2,1,0:T(8,128)(2,1)} %param.35) | copy-start | bytes 2359300
  206.7 5.8 copy-start.3
  207.3 4.7 collective-permute-start
  215.4 152.8 %copy-start.6 = (bf16[768,1024]{1,0:T(8,128)(2,1)}, bf16[768,1024]{1,0:T(8,128)(2,1)S(1)}, u32[]{:S(2)}) copy-start(bf16[768,1024]{1,0:T(8,128)(2,1)S(1)} %get-tuple-element.58) | copy-start | bytes 4718596
  235.2 39.5 %copy-start.41 = (bf16[128,2048]{1,0:T(8,128)(2,1)S(1)}, bf16[128,2048]{1,0:T(8,128)(2,1)}, u32[]{:S(2)}) copy-start(bf16[128,2048]{1,0:T(8,128)(2,1)} %param.41) | copy-start | bytes 1572868
  235.2 424.6 %all-gather.13.cloned.1.call-start = ((), (), s32[]{:S(2)}) async-start(), calls=%async_computation.9 | async-start | bytes 28835840 | tf_op jit(solution)/shard_map/all_gather | solution.py:56
  236.0 673.6 %all-reduce.20.cloned.1.call-start = ((), (), s32[]{:S(2)}) async-start(), calls=%async_computation.16 | async-start | bytes 14155776 | tf_op jit(solution)/shard_map/psum | solution.py:228
  352.3 15.8 copy-start.28
  368.2 148.1 %copy-start.14 = (bf16[128,2048]{1,0:T(8,128)(2,1)S(1)}, bf16[128,2048]{1,0:T(8,128)(2,1)}, u32[]{:S(2)}) copy-start(bf16[128,2048]{1,0:T(8,128)(2,1)} %param.37) | copy-start | bytes 1572868
  395.0 126.0 %copy-start.16 = (bf16[768,128]{1,0:T(8,128)(2,1)}, bf16[768,128]{1,0:T(8,128)(2,1)S(1)}, u32[]{:S(2)}) copy-start(bf16[768,128]{1,0:T(8,128)(2,1)S(1)} %all-reduce.21) | copy-start | bytes 589828
  521.1 5.2 copy-start.21
  521.1 5.2 copy-start.26
  706.4 5.8 copy-start.62
  738.8 10.5 slice-start.5
  738.9 637.1 %all-reduce.16.cloned.1.call-start = ((), (), s32[]{:S(2)}) async-start(), calls=%async_computation.14 | async-start | bytes 23330816 | tf_op jit(solution)/shard_map/psum | solution.py:289
  740.0 9.3 slice-start.6
  743.7 5.7 copy-start.18
  749.4 160.2 %copy-start.22 = (f32[768,128]{1,0:T(8,128)S(1)}, f32[768,128]{1,0:T(8,128)}, u32[]{:S(2)}) copy-start(f32[768,128]{1,0:T(8,128)} %compare_convert_fusion) | copy-start | bytes 1179652
  914.2 5.1 slice-start
  914.5 5.3 copy-start.8
  922.7 7.8 slice-start.2
  931.8 7.2 copy-start.46
  931.8 7.2 copy-start.48
  931.8 7.2 copy-start.50
  931.8 7.2 copy-start.54
  931.8 7.2 copy-start.55
  933.4 5.5 collective-permute-start.1
  946.3 22.0 %copy-start.44 = (f32[768]{0:T(1024)S(1)}, f32[768]{0:T(1024)}, u32[]{:S(2)}) copy-start(f32[768]{0:T(1024)} %copy-done.43) | copy-start | bytes 9220
  946.3 22.0 %copy-start.52 = (f32[2048]{0:T(1024)S(1)}, f32[2048]{0:T(1024)}, u32[]{:S(2)}) copy-start(f32[2048]{0:T(1024)} %copy-done.51) | copy-start | bytes 24580
  974.4 446.6 %reduce-scatter.2.cloned.1.call-start = ((), (), s32[]{:S(2)}) async-start(), calls=%async_computation.11 | async-start | bytes 4718592 | tf_op jit(solution)/shard_map/reduce_scatter | solution.py:188
  988.8 587.9 %all-reduce.14.cloned.1.call-start = ((), (), s32[]{:S(2)}) async-start(), calls=%async_computation.13 | async-start | bytes 12582912 | tf_op jit(solution)/shard_map/psum | solution.py:266
  1004.7 817.5 %all-reduce.18.cloned.1.call-start = ((), (), s32[]{:S(2)}) async-start(), calls=%async_computation.15 | async-start | bytes 23330816 | tf_op jit(solution)/shard_map/psum | solution.py:288
  1376.0 45.0 %copy-start.42 = (bf16[128,2048]{1,0:T(8,128)(2,1)S(1)}, bf16[128,2048]{1,0:T(8,128)(2,1)}, u32[]{:S(2)}) copy-start(bf16[128,2048]{1,0:T(8,128)(2,1)} %param.41) | copy-start | bytes 1572868
  1424.1 152.6 %copy-start.36 = (bf16[2048,128]{1,0:T(8,128)(2,1)S(1)}, bf16[2048,128]{1,0:T(8,128)(2,1)}, u32[]{:S(2)}) copy-start(bf16[2048,128]{1,0:T(8,128)(2,1)} %param.34) | copy-start | bytes 1572868
  1630.3 41.8 %all-to-all-start.3 = ((bf16[4,192,1024]{2,1,0:T(8,128)(2,1)}), bf16[4,192,1024]{2,1,0:T(8,128)(2,1)}, u32[]{:S(2)}, u32[]{:S(2)}) async-start(bf16[4,192,1024]{2,1,0:T(8,128)(2,1)} %get-tuple-element.74), calls=%async_computation.4 | async-start | bytes 3145728 | tf_op jit(solution)/shard_map/all_to_all | solution.py:282
  (38 other events, 115.8 us)
Sparse Core Ops, SparseCore 0:
  61.9 46.0 all-gather.6
  109.6 82.0 all-gather.8
  193.3 34.4 all-gather.10
  229.8 44.9 all-gather.16
  276.2 76.1 all-gather.14
  354.6 161.6 all-reduce.11
  518.0 141.8 all-gather.12
  739.0 170.5 all-reduce.19
  974.5 401.4 all-reduce.15
  1378.7 42.2 reduce-scatter.1
  1423.5 153.2 all-reduce.13
  1580.1 242.0 all-reduce.17
